TPU v7x, 512 devices: a whole 4x4x16 slice. The times are simulated.
512 devices in a mesh: net: 16 (over z), seg: 8 (over y, core), corner: 4 (over x).
Axes of the slice: x: 4, y: 4, z: 16, core: 2. Of those that a mesh axis runs over, the one named last changes fastest.
Arguments:
- tile_values: bfloat16 [8192, 128, 1024], P(('net', 'seg', 'corner')), may hold values from -48 to 48
- tile_coords: int32 [8192, 3], P(('net', 'seg', 'corner')), may hold values from 0 to 511, as said below
- tile_count: int32 [512], P(('net', 'seg', 'corner')), may hold values from 12 to 16, as said below
- owner_map: int32 [512], P('net'), may hold values from 0 to 511, as said below
- corner_factor: bfloat16 [64, 256], P('corner')
- seg_factor: bfloat16 [65536, 256], P(('seg', 'net'))
Outputs:
- net_factor: float32 [65536, 256], P(('net', 'seg', 'corner'))
Inputs may be any that keep to these rules, and one draw needn't show every extreme that they name: `tile_coords`: row t of device d gives a corner block within the corner range stored by d's corner index, a net block that owner_map assigns to an owner slot of d's net index, and a segment block within the segment range of d's seg index. Among a device's 16 rows at most 2 name segment blocks stored by any one device of the net axis, and on every device two live rows name segment blocks stored by the same device of the net axis. The first tile_count[d] rows of device d are live; the others are ignored. `owner_map`: A permutation of the 512 net blocks.
All inputs are finite; a program needn't handle non-finite values.
Results may differ from a plain program's by a relative error of at most 0.0058.
The roundings to bfloat16 on the way count: a program that leaves them out, or rounds other values in their place, can miss the bound.
Values may be sent and summed in bfloat16 or wider, within the bound.
No kernel may reach another device: no remote copies, remote signals or barrier semaphores. Data moves between devices by JAX's collectives and lax.ppermute only.
A program may use at most 64 MiB of HBM per device.

v0:
```python
import jax
import jax.numpy as jnp
from jax import lax
from jax.sharding import PartitionSpec as P

CBLK = 8
GRP = 4


def solve_rows(gram, mttkrp):
    cholesky_low = jnp.linalg.cholesky(gram)
    forward = lax.linalg.triangular_solve(cholesky_low, mttkrp.T, left_side=True, lower=True)
    backward = lax.linalg.triangular_solve(
        cholesky_low, forward, left_side=True, lower=True, transpose_a=True
    )
    return backward.T


def contract(packed):
    values, corner_rows, seg_rows = packed
    khatri = (
        corner_rows.astype(jnp.float32)[:, :, None, :] * seg_rows.astype(jnp.float32)[:, None, :, :]
    ).astype(jnp.bfloat16)
    khatri = khatri.reshape(values.shape[0], values.shape[2], corner_rows.shape[2])
    return jnp.einsum("tnj,tjr->tnr", values, khatri, preferred_element_type=jnp.float32)


def body(tile_values, tile_coords, tile_count, owner_map, corner_factor, seg_factor):
    slot_total = tile_values.shape[0]
    net_rows = tile_values.shape[1]
    columns = corner_factor.shape[1]
    seg_width = tile_values.shape[2] // CBLK
    held_blocks = seg_factor.shape[0] // seg_width
    net_devices = lax.axis_size("net")
    corner_local = tile_coords[:, 0] - lax.axis_index("corner") * (corner_factor.shape[0] // CBLK)
    seg_local = tile_coords[:, 2] - lax.axis_index("seg") * (held_blocks * net_devices)
    corner_sel = jnp.take(corner_factor.reshape(-1, CBLK, columns), corner_local, axis=0)
    gathered = lax.all_gather(seg_factor, "net", axis=0, tiled=True)
    seg_sel = jnp.take(gathered.reshape(-1, seg_width, columns), seg_local, axis=0)
    groups = slot_total // GRP
    partial_value = lax.map(
        contract,
        (
            tile_values.reshape(groups, GRP, net_rows, -1),
            corner_sel.reshape(groups, GRP, CBLK, columns),
            seg_sel.reshape(groups, GRP, seg_width, columns),
        ),
    )
    partial_value = partial_value.reshape(slot_total, net_rows * columns)
    live_mask = jnp.arange(slot_total, dtype=jnp.int32) < tile_count[0]
    member = ((tile_coords[:, 1][:, None] == owner_map[None, :]) & live_mask[:, None]).astype(
        jnp.float32
    )
    summed = jnp.dot(
        member.T, partial_value, precision=lax.Precision.HIGHEST, preferred_element_type=jnp.float32
    )
    mttkrp = lax.psum_scatter(
        summed.reshape(net_rows * lax.axis_size(("seg", "corner")), columns),
        ("seg", "corner"),
        scatter_dimension=0,
        tiled=True,
    )
    corner_part = jnp.dot(corner_factor.T, corner_factor, preferred_element_type=jnp.float32)
    seg_part = jnp.dot(seg_factor.T, seg_factor, preferred_element_type=jnp.float32)
    seg_gram = lax.psum(seg_part, ("net", "seg"))
    corner_gram = lax.psum(corner_part, "corner")
    return solve_rows(corner_gram * seg_gram, mttkrp)


def solution(mesh):
    return jax.shard_map(
        body,
        mesh=mesh,
        in_specs=(
            P(("net", "seg", "corner"), None, None),
            P(("net", "seg", "corner"), None),
            P(("net", "seg", "corner")),
            P("net"),
            P("corner", None),
            P(("seg", "net"), None),
        ),
        out_specs=P(("net", "seg", "corner"), None),
        check_vma=False,
    )
```

profile of v0, /device:TPU:8, one launch (start us, length us, event | category | flops | bytes accessed | tf_op | source)
XLA Modules:
  0.0 481.0 jit_solution(18225845388589294858)
XLA Ops:
  7.4 0.7 all-gather.2.cloned.1.call-update
  8.1 2.1 fusion.23
  10.3 1.0 fusion.22
  11.4 0.7 slice_bitcast_fusion.6
  12.1 0.8 and_reduce_fusion
  12.8 0.1 broadcast_in_dim.38
  12.9 0.1 broadcast_in_dim.41
  13.7 0.6 gather_fusion
  14.3 0.1 broadcast_select_fusion.1
  14.3 79.2 %all-gather.2.cloned.1.call-done = bf16[8192,256]{1,0:T(8,128)(2,1)} async-done(((bf16[512,256]{1,0:T(8,128)(2,1)}), bf16[8192,256]{1,0:T(8,128)(2,1)}) %all-gather.2.cloned.1.call-update) | async-done | bytes 4194320 | tf_op jit(solution)/shard_map/all_gather | solution.py:38
  93.5 2.8 gather_fusion.1
  96.4 0.2 broadcast_select_fusion
  96.5 12.6 %while.11 = (s32[]{:T(128)}, f32[4,4,128,256]{3,2,1,0:T(8,128)}, bf16[4,4,128,1024]{3,2,1,0:T(8,128)(2,1)}, bf16[4,4,8,256]{3,2,1,0:T(8,128)(2,1)S(1)}, bf16[4,4,128,256]{3,2,1,0:T(8,128)(2,1)S(1)}, /*index=5*/s32[]{:T(128)}) while((s32[]{:T(128)}, f32[4,4,128,256]{3,2,1,0:T(8,128)}, bf16[4,4,128,1024]{3,2,1,0:T(8,128)(2,1)}, ...), condition=%wide.region_7.8_spmd, body=%wide.region_6.7_spmd.sunk | while | flops 270671872 | bytes 7160917 | solution.py:41
  96.6 0.6 multiply_convert_fusion.2
  97.2 2.5 fusion.43
  99.7 0.6 multiply_convert_fusion.2
  100.3 2.5 fusion.43
  102.9 0.6 multiply_convert_fusion.2
  103.5 2.5 fusion.43
  106.0 0.6 multiply_convert_fusion.2
  106.6 2.5 fusion.43
  109.1 2.8 copy.13
  111.9 3.5 fusion.15
  115.5 4.9 %reshape.80 = f32[4096,256]{1,0:T(8,128)} reshape(f32[32,32768]{1,0:T(8,128)} %fusion.15) | data formatting | bytes 8388608 | tf_op jit(solution)/shard_map/reshape | solution.py:58
  120.4 232.0 %all-reduce.6.cloned.1.call-done = f32[256,256]{0,1:T(8,128)} async-done(((f32[256,256]{0,1:T(8,128)}), f32[256,256]{0,1:T(8,128)}) %all-reduce.6.cloned.1.call-update) | async-done | bytes 262160 | tf_op jit(solution)/shard_map/psum | solution.py:65
  352.4 56.2 %all-reduce.4.cloned.1.call-done = f32[256,256]{0,1:T(8,128)} async-done(((f32[256,256]{0,1:T(8,128)}), f32[256,256]{0,1:T(8,128)}) %all-reduce.4.cloned.1.call-update) | async-done | bytes 262160 | tf_op jit(solution)/shard_map/psum | solution.py:66
  408.6 1.1 mul.24
  409.6 0.1 copy.9
  409.8 11.7 %cholesky.50 = f32[128,128]{1,0:T(8,128)S(1)} custom-call(f32[128,128]{1,0:T(8,128)S(1)} %cholesky.118), custom_call_target="Cholesky" | custom-call | tf_op jit(solution)/shard_map/jit(cholesky)/cholesky | solution.py:11
  421.6 9.8 %custom-call.16 = f32[1,128,128]{1,2,0:T(8,128)S(1)} custom-call(f32[1,128,128]{2,1,0:T(8,128)S(1)} %get-tuple-element.68), custom_call_target="InvertDiagBlocksLowerTriangular" | custom-call | tf_op jit(solution)/shard_map/jit(cholesky)/cholesky | solution.py:11
  431.4 0.2 constant_dynamic-update-slice_fusion.1
  431.6 0.3 convolution_subtract_fusion.2
  431.9 11.7 %cholesky.105 = f32[128,128]{1,0:T(8,128)S(1)} custom-call(f32[128,128]{1,0:T(8,128)S(1)} %convolution_subtract_fusion.2), custom_call_target="Cholesky" | custom-call | tf_op jit(solution)/shard_map/jit(cholesky)/cholesky | solution.py:11
  443.7 0.7 compare_reduce_fusion
  445.6 0.1 triangular_solve.66
  445.7 3.9 while.12
  445.7 0.6 fusion.44
  446.3 1.3 bitcast_dynamic-update-slice_fusion.2
  447.7 0.6 fusion.44
  448.3 1.3 bitcast_dynamic-update-slice_fusion.2
  449.6 19.9 %custom-call.17 = f32[2,128,128]{1,2,0:T(8,128)S(1)} custom-call(f32[2,128,128]{2,1,0:T(8,128)S(1)} %get-tuple-element.40), custom_call_target="InvertDiagBlocksLowerTriangular" | custom-call | tf_op jit(solution)/shard_map/triangular_solve | solution.py:13
  469.5 1.1 fusion.5
  470.7 1.1 convolution_subtract_fusion.1
  471.8 0.3 fusion.12
  472.1 0.2 fusion.11
  472.3 0.3 convolution_subtract_fusion
  472.6 0.2 fusion.10
  472.8 0.8 copy.10
  (35 shorter events, 0.6 us)
Async XLA Ops:
  7.4 2.9 copy-start
  7.4 86.2 %all-gather.2.cloned.1.call-start = ((), (), s32[]{:S(2)}) async-start(), calls=%async_computation.3 | async-start | bytes 4456448 | tf_op jit(solution)/shard_map/all_gather | solution.py:38
  8.1 344.3 %all-reduce.6.cloned.1.call-start = ((), (), s32[]{:S(2)}) async-start(), calls=%async_computation.2 | async-start | bytes 524288 | tf_op jit(solution)/shard_map/psum | solution.py:65
  10.3 398.3 %all-reduce.4.cloned.1.call-start = ((), (), s32[]{:S(2)}) async-start(), calls=%async_computation.1 | async-start | bytes 524288 | tf_op jit(solution)/shard_map/psum | solution.py:66
  11.3 458.2 %reduce-scatter.2.cloned.1.call-start = ((), (), s32[]{:S(2)}) async-start(), calls=%async_computation.4 | async-start | bytes 4325376 | tf_op jit(solution)/shard_map/reduce_scatter | solution.py:57
  109.1 2.8 copy-start.1
Sparse Core Ops, SparseCore 0:
  10.3 83.2 all-gather.1
  120.5 101.2 reduce-scatter.1
Sparse Core Ops, SparseCore 1:
  12.4 339.9 all-reduce.5
  354.7 53.8 all-reduce.3
where the time goes:
time: 482 us; the launch traced here: 481 us
  waiting for transfers between devices  368 us (76%)
  other arithmetic  58.6 us (12%)
  matrix products  20.2 us (4%)
  between operations  17 us (4%)
  local copies, waits for them, and re-layouts  16.8 us (3%)
    psum x1, waiting for transfers between devices, body(): seg_gram = lax.psum(seg_part, ('net', 'seg'))  232 us
    all_gather x1, waiting for transfers between devices, body(): gathered = lax.all_gather(seg_factor, 'net', axis=0, tiled=True)  79.2 us
    psum x1, waiting for transfers between devices, body(): corner_gram = lax.psum(corner_part, 'corner')  56.2 us
    another operation x6, other arithmetic, solve_rows(): cholesky_low = jnp.linalg.cholesky(gram)  34 us
    another operation x3, other arithmetic, solve_rows(): lax.linalg.triangular_solve(cholesky_low, forward, left_side=True, lower=...  19.9 us
    dot_general x4, matrix products, contract(): jnp.einsum('tnj,tjr->tnr', values, khatri, preferred_element_type=jnp.flo...  9.96 us
  transfers between devices with their start and end apart: 4, of which 3 were waited for; matrix products, arithmetic and copies ran while one was open for 19% of the time, Pallas kernels for 0%

commit v1 on v0

--- a/solution.py
+++ b/solution.py
@@ -35,7 +35,8 @@
     corner_local = tile_coords[:, 0] - lax.axis_index("corner") * (corner_factor.shape[0] // CBLK)
     seg_local = tile_coords[:, 2] - lax.axis_index("seg") * (held_blocks * net_devices)
     corner_sel = jnp.take(corner_factor.reshape(-1, CBLK, columns), corner_local, axis=0)
-    gathered = lax.all_gather(seg_factor, "net", axis=0, tiled=True)
+    copies = jnp.concatenate([seg_factor] * lax.axis_size("net"), axis=0)
+    gathered = lax.all_to_all(copies, "net", 0, 0, tiled=True)
     seg_sel = jnp.take(gathered.reshape(-1, seg_width, columns), seg_local, axis=0)
     groups = slot_total // GRP
     partial_value = lax.map(

time: 482 us -> 566 us (1.17)
  waiting for transfers between devices: 368 us -> 430 us
  starting transfers between devices: 0.13 us -> 15.5 us
  local copies, waits for them, and re-layouts: 16.8 us -> 26.1 us
    all_to_all x0 -> x1, waiting for transfers between devices: none -> 180 us  [body(): gathered = lax.all_to_all(copies, 'net', 0, 0, tiled=True)]
    all_gather x1 -> x0, waiting for transfers between devices: 79.2 us -> none  [body(): gathered = lax.all_gather(seg_factor, 'net', axis=0, tiled=True)]
    psum x1, waiting for transfers between devices: 232 us -> 193 us  [body(): seg_gram = lax.psum(seg_part, ('net', 'seg'))]
    all_to_all x0 -> x1, starting transfers between devices: none -> 15.4 us  [body(): gathered = lax.all_to_all(copies, 'net', 0, 0, tiled=True)]
    unnamed x5 -> x26, local copies, waits for them, and re-layouts: 2.84 us -> 12.8 us
  transfers between devices with their start and end apart: 4 -> 4, of which waited for: 3 -> 3; matrix products, arithmetic and copies ran while one was open for 19% -> 16% of each run, Pallas kernels for 0% -> 0%
where the time goes in v1:
time: 566 us; the launch traced here: 565 us
  waiting for transfers between devices  430 us (76%)
  other arithmetic  57.8 us (10%)
  local copies, waits for them, and re-layouts  26.1 us (5%)
  matrix products  19.2 us (3%)
  between operations  17.1 us (3%)
  starting transfers between devices  15.5 us (3%)
    psum x1, waiting for transfers between devices, body(): seg_gram = lax.psum(seg_part, ('net', 'seg'))  193 us
    all_to_all x1, waiting for transfers between devices, body(): gathered = lax.all_to_all(copies, 'net', 0, 0, tiled=True)  180 us
    psum x1, waiting for transfers between devices, body(): corner_gram = lax.psum(corner_part, 'corner')  56.5 us
    another operation x6, other arithmetic, solve_rows(): cholesky_low = jnp.linalg.cholesky(gram)  34 us
    another operation x3, other arithmetic, solve_rows(): lax.linalg.triangular_solve(cholesky_low, forward, left_side=True, lower=...  19.9 us
    all_to_all x1, starting transfers between devices, body(): gathered = lax.all_to_all(copies, 'net', 0, 0, tiled=True)  15.4 us
    unnamed x26, local copies, waits for them, and re-layouts  12.8 us
  transfers between devices with their start and end apart: 4, of which 3 were waited for; matrix products, arithmetic and copies ran while one was open for 16% of the time, Pallas kernels for 0%

profile of v1, /device:TPU:8, one launch (start us, length us, event | category | flops | bytes accessed | tf_op | source)
XLA Modules:
  0.0 565.3 jit_solution(1328085299285931321)
XLA Ops:
  7.4 1.0 constant_dynamic-update-slice_fusion.15
  8.4 1.0 constant_dynamic-update-slice_fusion.14
  9.4 1.0 constant_dynamic-update-slice_fusion.13
  10.4 1.0 constant_dynamic-update-slice_fusion.12
  11.3 1.0 constant_dynamic-update-slice_fusion.11
  12.3 1.0 constant_dynamic-update-slice_fusion.10
  13.3 1.0 constant_dynamic-update-slice_fusion.9
  14.3 1.0 constant_dynamic-update-slice_fusion.8
  15.5 2.0 copy-done.2
  17.4 15.4 %all-to-all-start = ((bf16[16,512,256]{2,1,0:T(8,128)(2,1)}), bf16[16,512,256]{2,1,0:T(8,128)(2,1)}, u32[]{:S(2)}, u32[]{:S(2)}) async-start(bf16[16,512,256]{2,1,0:T(8,128)(2,1)} %bitcast.90), calls=%async_computation | async-start | bytes 8388608 | tf_op jit(solution)/shard_map/all_to_all | solution.py:39
  32.9 1.0 fusion.23
  33.9 0.9 fusion.22
  35.8 0.6 gather_fusion
  36.5 179.9 %all-to-all-done = bf16[16,512,256]{2,1,0:T(8,128)(2,1)} async-done(((bf16[16,512,256]{2,1,0:T(8,128)(2,1)}), bf16[16,512,256]{2,1,0:T(8,128)(2,1)}, u32[]{:S(2)}, u32[]{:S(2)}) %all-to-all-start) | async-done | bytes 4194336 | tf_op jit(solution)/shard_map/all_to_all | solution.py:39
  216.5 2.8 gather_fusion.1
  219.4 12.6 %while.11 = (s32[]{:T(128)}, f32[4,4,128,256]{3,2,1,0:T(8,128)}, bf16[4,4,128,1024]{3,2,1,0:T(8,128)(2,1)}, bf16[4,4,8,256]{3,2,1,0:T(8,128)(2,1)S(1)}, bf16[4,4,128,256]{3,2,1,0:T(8,128)(2,1)S(1)}, /*index=5*/s32[]{:T(128)}) while((s32[]{:T(128)}, f32[4,4,128,256]{3,2,1,0:T(8,128)}, bf16[4,4,128,1024]{3,2,1,0:T(8,128)(2,1)}, ...), condition=%wide.region_7.8_spmd, body=%wide.region_6.7_spmd.sunk | while | flops 270671872 | bytes 7160909 | solution.py:42
  219.5 0.6 multiply_convert_fusion.2
  220.1 2.5 fusion.43
  222.7 0.6 multiply_convert_fusion.2
  223.3 2.5 fusion.43
  225.9 0.6 multiply_convert_fusion.2
  226.5 2.5 fusion.43
  229.0 0.6 multiply_convert_fusion.2
  229.6 2.5 fusion.43
  232.1 2.8 copy.13
  234.9 3.5 fusion.15
  238.4 4.9 reshape.83
  243.3 193.0 %all-reduce.6.cloned.1.call-done = f32[256,256]{0,1:T(8,128)} async-done(((f32[256,256]{0,1:T(8,128)}), f32[256,256]{0,1:T(8,128)}) %all-reduce.6.cloned.1.call-update) | async-done | bytes 262160 | tf_op jit(solution)/shard_map/psum | solution.py:66
  436.4 56.5 %all-reduce.4.cloned.1.call-done = f32[256,256]{0,1:T(8,128)} async-done(((f32[256,256]{0,1:T(8,128)}), f32[256,256]{0,1:T(8,128)}) %all-reduce.4.cloned.1.call-update) | async-done | bytes 262160 | tf_op jit(solution)/shard_map/psum | solution.py:67
  492.8 1.1 mul.24
  494.1 11.7 %cholesky.50 = f32[128,128]{1,0:T(8,128)S(1)} custom-call(f32[128,128]{1,0:T(8,128)S(1)} %cholesky.118), custom_call_target="Cholesky" | custom-call | tf_op jit(solution)/shard_map/jit(cholesky)/cholesky | solution.py:11
  505.9 9.8 %custom-call.16 = f32[1,128,128]{1,2,0:T(8,128)S(1)} custom-call(f32[1,128,128]{2,1,0:T(8,128)S(1)} %get-tuple-element.68), custom_call_target="InvertDiagBlocksLowerTriangular" | custom-call | tf_op jit(solution)/shard_map/jit(cholesky)/cholesky | solution.py:11
  515.7 0.2 constant_dynamic-update-slice_fusion.17
  515.9 0.3 convolution_subtract_fusion.2
  516.2 11.7 %cholesky.105 = f32[128,128]{1,0:T(8,128)S(1)} custom-call(f32[128,128]{1,0:T(8,128)S(1)} %convolution_subtract_fusion.2), custom_call_target="Cholesky" | custom-call | tf_op jit(solution)/shard_map/jit(cholesky)/cholesky | solution.py:11
  527.9 0.7 compare_reduce_fusion
  529.9 3.9 while.12
  530.0 0.6 fusion.44
  530.6 1.3 bitcast_dynamic-update-slice_fusion.2
  531.9 0.6 fusion.44
  532.5 1.3 bitcast_dynamic-update-slice_fusion.2
  533.9 19.9 %custom-call.17 = f32[2,128,128]{1,2,0:T(8,128)S(1)} custom-call(f32[2,128,128]{2,1,0:T(8,128)S(1)} %get-tuple-element.40), custom_call_target="InvertDiagBlocksLowerTriangular" | custom-call | tf_op jit(solution)/shard_map/triangular_solve | solution.py:13
  553.8 1.1 fusion.5
  554.9 1.1 convolution_subtract_fusion.1
  556.1 0.3 fusion.12
  556.4 0.2 fusion.11
  556.6 0.3 convolution_subtract_fusion
  557.1 0.8 copy.10
  (56 shorter events, 1.6 us)
Async XLA Ops:
  7.4 26.6 %copy-start = (bf16[16,256]{1,0:T(8,128)(2,1)S(1)}, bf16[16,256]{1,0:T(8,128)(2,1)}, u32[]{:S(2)}) copy-start(bf16[16,256]{1,0:T(8,128)(2,1)} %param.12) | copy-start | bytes 24580
  7.4 7.9 %copy-start.1 = (bf16[512,256]{1,0:T(8,128)(2,1)S(1)}, bf16[512,256]{1,0:T(8,128)(2,1)}, u32[]{:S(2)}) copy-start(bf16[512,256]{1,0:T(8,128)(2,1)} %param.13) | copy-start | bytes 786436
  15.5 2.0 copy-start.2
  17.4 17.5 %copy-start.4 = (s32[16,3]{0,1:T(4,128)S(1)}, s32[16,3]{0,1:T(4,128)}, u32[]{:S(2)}) copy-start(s32[16,3]{0,1:T(4,128)} %param.9) | copy-start | bytes 580
  17.4 199.0 %all-to-all-start = ((bf16[16,512,256]{2,1,0:T(8,128)(2,1)}), bf16[16,512,256]{2,1,0:T(8,128)(2,1)}, u32[]{:S(2)}, u32[]{:S(2)}) async-start(bf16[16,512,256]{2,1,0:T(8,128)(2,1)} %bitcast.90), calls=%async_computation | async-start | bytes 8388608 | tf_op jit(solution)/shard_map/all_to_all | solution.py:39
  32.8 403.5 %all-reduce.6.cloned.1.call-start = ((), (), s32[]{:S(2)}) async-start(), calls=%async_computation.3 | async-start | bytes 524288 | tf_op jit(solution)/shard_map/psum | solution.py:66
  33.9 459.0 %all-reduce.4.cloned.1.call-start = ((), (), s32[]{:S(2)}) async-start(), calls=%async_computation.2 | async-start | bytes 524288 | tf_op jit(solution)/shard_map/psum | solution.py:67
  34.9 518.9 %reduce-scatter.2.cloned.1.call-start = ((), (), s32[]{:S(2)}) async-start(), calls=%async_computation.4 | async-start | bytes 4325376 | tf_op jit(solution)/shard_map/reduce_scatter | solution.py:58
  232.1 2.8 copy-start.3
Sparse Core Ops, SparseCore 0:
  37.5 398.8 all-reduce.5
  438.8 54.0 all-reduce.3
Sparse Core Ops, SparseCore 1:
  243.4 104.5 reduce-scatter.1

commit v2 on v0

--- a/solution.py
+++ b/solution.py
@@ -63,7 +63,7 @@
     corner_part = jnp.dot(corner_factor.T, corner_factor, preferred_element_type=jnp.float32)
     seg_part = jnp.dot(seg_factor.T, seg_factor, preferred_element_type=jnp.float32)
     seg_gram = lax.psum(seg_part, ("net", "seg"))
-    corner_gram = lax.psum(corner_part, "corner")
+    corner_gram = jnp.sum(lax.all_gather(corner_part, "corner"), axis=0)
     return solve_rows(corner_gram * seg_gram, mttkrp)
 
 

time: 482 us -> 426 us (0.88)
  the two profiles are of different devices: /device:TPU:8 before, /device:TPU:1 now
where the time goes in v2:
time: 426 us; the launch traced here: 425 us
  waiting for transfers between devices  311 us (73%)
  other arithmetic  59.8 us (14%)
  matrix products  20.2 us (5%)
  local copies, waits for them, and re-layouts  17 us (4%)
  between operations  16.7 us (4%)
    psum x1, waiting for transfers between devices, body(): seg_gram = lax.psum(seg_part, ('net', 'seg'))  228 us
    all_gather x1, waiting for transfers between devices, body(): gathered = lax.all_gather(seg_factor, 'net', axis=0, tiled=True)  72 us
    another operation x6, other arithmetic, solve_rows(): cholesky_low = jnp.linalg.cholesky(gram)  34 us
    another operation x3, other arithmetic, solve_rows(): lax.linalg.triangular_solve(cholesky_low, forward, left_side=True, lower=...  19.9 us
    all_gather x1, waiting for transfers between devices, body(): corner_gram = jnp.sum(lax.all_gather(corner_part, 'corner'), axis=0)  10.6 us
    dot_general x4, matrix products, contract(): jnp.einsum('tnj,tjr->tnr', values, khatri, preferred_element_type=jnp.flo...  9.96 us
  transfers between devices with their start and end apart: 4, of which 3 were waited for; matrix products, arithmetic and copies ran while one was open for 22% of the time, Pallas kernels for 0%

profile of v2, /device:TPU:1, one launch (start us, length us, event | category | flops | bytes accessed | tf_op | source)
XLA Modules:
  0.0 425.2 jit_solution(6976329644886090397)
XLA Ops:
  7.4 0.7 all-gather.4.cloned.1.call-update
  8.1 0.9 fusion.22
  9.2 2.0 fusion.23
  11.3 0.7 slice_bitcast_fusion.6
  12.0 0.8 and_reduce_fusion
  12.8 0.1 broadcast_in_dim.38
  13.6 0.6 gather_fusion
  14.2 0.1 broadcast_select_fusion.1
  14.3 72.0 %all-gather.4.cloned.1.call-done = bf16[8192,256]{1,0:T(8,128)(2,1)} async-done(((bf16[512,256]{1,0:T(8,128)(2,1)}), bf16[8192,256]{1,0:T(8,128)(2,1)}) %all-gather.4.cloned.1.call-update) | async-done | bytes 4194320 | tf_op jit(solution)/shard_map/all_gather | solution.py:38
  86.3 2.8 gather_fusion.1
  89.1 0.2 broadcast_select_fusion
  89.3 12.6 %while.11 = (s32[]{:T(128)}, f32[4,4,128,256]{3,2,1,0:T(8,128)}, bf16[4,4,128,1024]{3,2,1,0:T(8,128)(2,1)}, bf16[4,4,8,256]{3,2,1,0:T(8,128)(2,1)S(1)}, bf16[4,4,128,256]{3,2,1,0:T(8,128)(2,1)S(1)}, /*index=5*/s32[]{:T(128)}) while((s32[]{:T(128)}, f32[4,4,128,256]{3,2,1,0:T(8,128)}, bf16[4,4,128,1024]{3,2,1,0:T(8,128)(2,1)}, ...), condition=%wide.region_7.8_spmd, body=%wide.region_6.7_spmd.sunk | while | flops 270671872 | bytes 7160917 | solution.py:41
  89.4 0.6 multiply_convert_fusion.2
  90.0 2.5 fusion.43
  92.5 0.6 multiply_convert_fusion.2
  93.1 2.5 fusion.43
  95.7 0.6 multiply_convert_fusion.2
  96.2 2.5 fusion.43
  98.8 0.6 multiply_convert_fusion.2
  99.4 2.5 fusion.43
  101.9 2.8 copy.15
  104.7 3.5 fusion.15
  108.2 5.0 %reshape.80 = f32[4096,256]{1,0:T(8,128)} reshape(f32[32,32768]{1,0:T(8,128)} %fusion.15) | data formatting | bytes 8388608 | tf_op jit(solution)/shard_map/reshape | solution.py:58
  113.3 10.6 %all-gather.6.cloned.1.call-done = f32[1024,256]{1,0:T(8,128)} async-done(((f32[256,256]{1,0:T(8,128)}), f32[1024,256]{1,0:T(8,128)}) %all-gather.6.cloned.1.call-update) | async-done | bytes 1048592 | tf_op jit(solution)/shard_map/all_gather | solution.py:66
  123.8 1.3 reduce_sum.9
  125.2 0.1 copy.11
  125.3 227.8 %all-reduce.3.cloned.1.call-done = f32[256,256]{0,1:T(8,128)} async-done(((f32[256,256]{0,1:T(8,128)}), f32[256,256]{0,1:T(8,128)}) %all-reduce.3.cloned.1.call-update) | async-done | bytes 262160 | tf_op jit(solution)/shard_map/psum | solution.py:65
  353.1 1.0 mul.24
  354.1 0.1 copy.12
  354.3 11.7 %cholesky.50 = f32[128,128]{1,0:T(8,128)S(1)} custom-call(f32[128,128]{1,0:T(8,128)S(1)} %cholesky.118), custom_call_target="Cholesky" | custom-call | tf_op jit(solution)/shard_map/jit(cholesky)/cholesky | solution.py:11
  366.1 9.8 %custom-call.16 = f32[1,128,128]{1,2,0:T(8,128)S(1)} custom-call(f32[1,128,128]{2,1,0:T(8,128)S(1)} %get-tuple-element.68), custom_call_target="InvertDiagBlocksLowerTriangular" | custom-call | tf_op jit(solution)/shard_map/jit(cholesky)/cholesky | solution.py:11
  375.9 0.2 constant_dynamic-update-slice_fusion.1
  376.1 0.3 convolution_subtract_fusion.2
  376.4 11.7 %cholesky.105 = f32[128,128]{1,0:T(8,128)S(1)} custom-call(f32[128,128]{1,0:T(8,128)S(1)} %convolution_subtract_fusion.2), custom_call_target="Cholesky" | custom-call | tf_op jit(solution)/shard_map/jit(cholesky)/cholesky | solution.py:11
  388.1 0.7 compare_reduce_fusion
  390.1 3.9 while.12
  390.1 0.6 fusion.44
  390.7 1.3 bitcast_dynamic-update-slice_fusion.2
  392.1 0.6 fusion.44
  392.7 1.3 bitcast_dynamic-update-slice_fusion.2
  394.0 19.9 %custom-call.17 = f32[2,128,128]{1,2,0:T(8,128)S(1)} custom-call(f32[2,128,128]{2,1,0:T(8,128)S(1)} %get-tuple-element.40), custom_call_target="InvertDiagBlocksLowerTriangular" | custom-call | tf_op jit(solution)/shard_map/triangular_solve | solution.py:13
  414.0 1.1 fusion.5
  415.1 1.1 convolution_subtract_fusion.1
  416.2 0.3 fusion.12
  416.5 0.2 fusion.11
  416.7 0.3 convolution_subtract_fusion
  417.0 0.2 fusion.10
  417.3 0.8 copy.13
  (37 shorter events, 0.8 us)
Async XLA Ops:
  7.4 0.8 copy-start
  7.4 78.9 %all-gather.4.cloned.1.call-start = ((), (), s32[]{:S(2)}) async-start(), calls=%async_computation.2 | async-start | bytes 4456448 | tf_op jit(solution)/shard_map/all_gather | solution.py:38
  8.1 115.8 %all-gather.6.cloned.1.call-start = ((), (), s32[]{:S(2)}) async-start(), calls=%async_computation.4 | async-start | bytes 1310720 | tf_op jit(solution)/shard_map/all_gather | solution.py:66
  9.1 344.0 %all-reduce.3.cloned.1.call-start = ((), (), s32[]{:S(2)}) async-start(), calls=%async_computation.1 | async-start | bytes 524288 | tf_op jit(solution)/shard_map/psum | solution.py:65
  11.2 402.7 %reduce-scatter.2.cloned.1.call-start = ((), (), s32[]{:S(2)}) async-start(), calls=%async_computation.3 | async-start | bytes 4325376 | tf_op jit(solution)/shard_map/reduce_scatter | solution.py:57
  101.9 2.8 copy-start.1
Sparse Core Ops, SparseCore 0:
  10.3 75.9 all-gather.3
  88.4 35.3 all-gather.5
  128.4 104.7 reduce-scatter.1
Sparse Core Ops, SparseCore 1:
  13.4 339.6 all-reduce.2
